TPU v7x, 32 devices: a whole 2x2x4 slice. The times are simulated.
32 devices in a mesh: row: 4 (over x, core), col: 8 (over z, y).
Axes of the slice: x: 2, y: 2, z: 4, core: 2. Of those that a mesh axis runs over, the one named last changes fastest.
Arguments:
- schur: float32 [4096, 4096], P('row', 'col'), may hold values from -6 to 6
- left_rot: float32 [8, 512, 512], P('row', 'col'), may hold values from -1 to 1, as said below
- right_rot: float32 [8, 512, 512], P('col', 'row'), may hold values from -1 to 1, as said below
- left_off: float32 [8, 512, 512], P('row', 'col'), may hold values from -1 to 1, as said below
- right_off: float32 [8, 512, 512], P('col', 'row'), may hold values from -1 to 1, as said below
Outputs:
- updated: float32 [4096, 4096], P('row', 'col')
Inputs may be any that keep to these rules, and one draw needn't show every extreme that they name: `left_rot`: each 512 x 512 block is orthogonal. `right_rot`: each 512 x 512 block is orthogonal. `left_off`: each 512 x 512 block is orthogonal. `right_off`: each 512 x 512 block is orthogonal.
All inputs are finite; a program needn't handle non-finite values.
Results may differ from a plain program's by a relative error of at most 0.00007.
Values sent between devices are 32-bit elements; how exact they have to be, the bound alone decides.
A program may use at most 64 MiB of HBM per device.

v0:
```python
import jax
import jax.numpy as jnp
from jax import lax
from jax.sharding import PartitionSpec as P


def passed_along(x, axis, by):
    size = lax.axis_size(axis)
    return lax.ppermute(x, axis, [(i, (i + by) % size) for i in range(size)])


def padded_2(cells, sides, width):
    for axis, dim in sides:
        count = lax.axis_size(axis)
        head = lax.slice_in_dim(cells, 0, width, axis=dim)
        tail = lax.slice_in_dim(cells, cells.shape[dim] - width, cells.shape[dim], axis=dim)
        cells = jnp.concatenate(
            [
                lax.ppermute(tail, axis, [(i, (i + 1) % count) for i in range(count)]),
                cells,
                lax.ppermute(head, axis, [((i + 1) % count, i) for i in range(count)]),
            ],
            axis=dim,
        )
    return cells


def apply_left(blocks, rotations):
    number = rotations.shape[0]
    window = rotations.shape[1]
    shaped = blocks.reshape(number, window, blocks.shape[1])
    result = jnp.einsum("kab,kac->kbc", rotations, shaped, precision=lax.Precision.HIGHEST)
    return result.reshape(number * window, blocks.shape[1])


def apply_right(blocks, rotations):
    number = rotations.shape[0]
    window = rotations.shape[1]
    shaped = blocks.reshape(blocks.shape[0], number, window)
    result = jnp.einsum("rka,kab->rkb", shaped, rotations, precision=lax.Precision.HIGHEST)
    return result.reshape(blocks.shape[0], number * window)


def body(schur, left_rot, right_rot, left_off, right_off):
    window = left_rot.shape[2]
    half_window = window // 2
    rows_here = schur.shape[0]
    cols_here = schur.shape[1]
    rotations = lax.all_gather(right_rot, "row", axis=1, tiled=True)
    matrix = apply_right(schur, rotations)
    rotations = lax.all_gather(left_rot, "col", axis=1, tiled=True)
    matrix = apply_left(matrix, rotations)
    rotations = lax.all_gather(right_off, "row", axis=1, tiled=True)
    following = passed_along(rotations[0][:, :half_window], "col", -1)
    padded = padded_2(matrix, (("col", 1),), half_window)
    leading = jnp.dot(
        padded[:, :window], rotations[0][:, half_window:], precision=lax.Precision.HIGHEST
    )
    middle = apply_right(padded[:, window:cols_here], rotations[1:])
    trailing = jnp.dot(
        padded[:, cols_here : cols_here + window], following, precision=lax.Precision.HIGHEST
    )
    matrix = jnp.concatenate([leading, middle, trailing], axis=1)
    rotations = lax.all_gather(left_off, "col", axis=1, tiled=True)
    following = passed_along(rotations[0][:, :half_window], "row", -1)
    padded = padded_2(matrix, (("row", 0),), half_window)
    leading = jnp.dot(
        rotations[0][:, half_window:].T, padded[:window], precision=lax.Precision.HIGHEST
    )
    middle = apply_left(padded[window:rows_here], rotations[1:])
    trailing = jnp.dot(
        following.T, padded[rows_here : rows_here + window], precision=lax.Precision.HIGHEST
    )
    return jnp.concatenate([leading, middle, trailing], axis=0)


def solution(mesh):
    return jax.shard_map(
        body,
        mesh=mesh,
        in_specs=(
            P("row", "col"),
            P("row", "col", None),
            P("col", "row", None),
            P("row", "col", None),
            P("col", "row", None),
        ),
        out_specs=P("row", "col"),
        check_vma=False,
    )
```

profile of v0, /device:TPU:1, one launch (start us, length us, event | category | flops | bytes accessed | tf_op | source)
XLA Modules:
  0.0 192.9 jit_solution(4929643086227449214)
XLA Ops:
  9.3 18.8 %all-gather.5.cloned.1.call-done = f32[1,512,512]{2,1,0:T(8,128)} async-done(((f32[1,128,512]{2,1,0:T(8,128)}), f32[1,512,512]{2,1,0:T(8,128)}) %all-gather.5.cloned.1.call-update) | async-done | bytes 1048592 | tf_op jit(solution)/shard_map/all_gather | solution.py:49
  28.1 9.3 %convolution_bitcast_fusion = f32[1024,1,512]{0,2,1:T(8,128)} fusion(f32[1024,512]{1,0:T(8,128)S(1)} %copy-done, f32[1,512,512]{2,1,0:T(8,128)} %all-gather.5.cloned.1.call-done), kind=kOutput, calls=%fused_computation.9 | convolution fusion | flops 3221225472 | bytes 5242880 | tf_op jit(solution)/shard_map/rka,kab->rkb/dot_general | solution.py:40
  37.3 3.0 %copy.7 = f32[1024,1,512]{2,0,1:T(8,128)} copy(f32[1024,1,512]{0,2,1:T(8,128)} %convolution_bitcast_fusion) | data formatting | bytes 4194304 | tf_op jit(solution)/shard_map/reshape;reshape | solution.py:31
  40.3 36.8 %all-gather.7.cloned.1.call-done = f32[2,512,512]{2,1,0:T(8,128)} async-done(((f32[2,64,512]{2,1,0:T(8,128)}), f32[2,512,512]{2,1,0:T(8,128)}) %all-gather.7.cloned.1.call-update) | async-done | bytes 2097168 | tf_op jit(solution)/shard_map/all_gather | solution.py:51
  77.1 5.8 %fusion.17 = f32[2,512,512]{1,2,0:T(8,128)S(1)} fusion(f32[2,512,512]{2,1,0:T(8,128)} %bitcast.31, f32[2,512,512]{2,1,0:T(8,128)} %all-gather.7.cloned.1.call-done), kind=kOutput, calls=%fused_computation.33 | convolution fusion | flops 3221225472 | bytes 6291456 | tf_op jit(solution)/shard_map/kab,kac->kbc/dot_general | solution.py:32
  82.8 1.4 fusion.16
  84.8 3.9 %collective-permute-start.1 = (f32[1024,256]{1,0:T(8,128)}, f32[1024,256]{1,0:T(8,128)}, u32[]{:S(2)}, u32[]{:S(2)}) collective-permute-start(f32[1024,256]{1,0:T(8,128)} %get-tuple-element.8), channel_id=1, source_target_pairs={{1,0},{2,1},{3,2},{4,3},{5,4},{6,5},{7,6},{0,7},{9,8},{10,9},{11,1... | collective-permute-start | bytes 3145736 | tf_op jit(solution)/shard_map/ppermute | solution.py:21
  88.7 7.5 %all-gather.9.cloned.1.call-done = f32[1,512,512]{2,1,0:T(8,128)} async-done(((f32[1,128,512]{2,1,0:T(8,128)}), f32[1,512,512]{2,1,0:T(8,128)}) %all-gather.9.cloned.1.call-update) | async-done | bytes 1048592 | tf_op jit(solution)/shard_map/all_gather | solution.py:53
  96.2 1.1 slice.68
  97.3 4.2 %collective-permute-start.2 = (f32[512,256]{1,0:T(8,128)S(1)}, f32[512,256]{1,0:T(8,128)S(1)}, u32[]{:S(2)}, u32[]{:S(2)}) collective-permute-start(f32[512,256]{1,0:T(8,128)S(1)} %slice.68), channel_id=1, source_target_pairs={{0,7},{1,0},{2,1},{3,2},{4,3},{5,4},{6,5},{7,6},{8,15},{9,8},{10,9... | collective-permute-start | bytes 1572872 | tf_op jit(solution)/shard_map/ppermute | solution.py:9
  101.5 42.8 %collective-permute-done = f32[1024,256]{1,0:T(8,128)} collective-permute-done((f32[1024,256]{1,0:T(8,128)S(1)}, f32[1024,256]{1,0:T(8,128)}, u32[]{:S(2)}, u32[]{:S(2)}) %collective-permute-start) | collective-permute-done | bytes 1048608 | tf_op jit(solution)/shard_map/ppermute | solution.py:19
  144.3 3.6 %fusion.2 = f32[1024,256]{0,1:T(8,128)S(1)} fusion(f32[1024,512]{1,0:T(8,128)} %bitcast.29, f32[1024,256]{1,0:T(8,128)} %collective-permute-done, f32[512,512]{1,0:T(8,128)} %bitcast.33), kind=kOutput, calls=%fused_computation.4 | convolution fusion | flops 1611137024 | bytes 4718592 | tf_op jit(solution)/shard_map/dot_general | solution.py:56
  147.9 6.7 %collective-permute-done.2 = f32[512,256]{1,0:T(8,128)S(1)} collective-permute-done((f32[512,256]{1,0:T(8,128)S(1)}, f32[512,256]{1,0:T(8,128)S(1)}, u32[]{:S(2)}, u32[]{:S(2)}) %collective-permute-start.2) | collective-permute-done | bytes 524320 | tf_op jit(solution)/shard_map/ppermute | solution.py:9
  154.6 3.3 %fusion = f32[1024,256]{0,1:T(8,128)S(1)} fusion(f32[512,256]{1,0:T(8,128)S(1)} %collective-permute-done.2, f32[1024,256]{1,0:T(8,128)} %collective-permute-done.1, f32[1024,512]{1,0:T(8,128)S(1)} %bitcast.30), kind=kOutput, calls=%fused_computation.1 | convolution fusion | flops 1611137024 | bytes 4718592 | tf_op jit(solution)/shard_map/dot_general | solution.py:60
  158.9 1.0 pad_maximum_fusion.14
  159.9 3.7 %collective-permute-start.3 = (f32[256,512]{0,1:T(8,128)}, f32[256,512]{0,1:T(8,128)}, u32[]{:S(2)}, u32[]{:S(2)}) collective-permute-start(f32[256,512]{0,1:T(8,128)} %get-tuple-element.5), channel_id=1, source_target_pairs={{0,8},{8,16},{16,24},{24,0},{1,9},{9,17},{17,25},{25,1},{2,10},{10... | collective-permute-start | bytes 1572872 | tf_op jit(solution)/shard_map/ppermute | solution.py:19
  163.6 4.1 %all-gather.11.cloned.1.call-done = f32[2,512,512]{2,1,0:T(8,128)} async-done(((f32[2,64,512]{2,1,0:T(8,128)}), f32[2,512,512]{2,1,0:T(8,128)}) %all-gather.11.cloned.1.call-update) | async-done | bytes 2097168 | tf_op jit(solution)/shard_map/all_gather | solution.py:64
  167.7 1.4 slice_bitcast_fusion.2
  170.9 1.9 convolution_bitcast_fusion.1
  172.7 2.1 %convolution_bitcast_fusion.3 = f32[256,512]{1,0:T(8,128)S(1)} fusion(f32[256,512]{0,1:T(8,128)} %collective-permute-done.3, f32[1024,256]{0,1:T(8,128)S(1)} %copy-done.4, f32[1024,256]{0,1:T(8,128)S(1)} %fusion.2, f32[512,512]{1,0:T(8,128)S(1)} %slice_bitcast_fusion.2), kind=kOutput, calls=%fused_computation.12 | convolution fusion | flops 805830656 | bytes 3670016 | tf_op jit(solution)/shard_map/dot_general | solution.py:67
  174.9 3.3 %collective-permute-done.5 = f32[512,256]{1,0:T(8,128)S(1)} collective-permute-done((f32[512,256]{1,0:T(8,128)S(1)}, f32[512,256]{1,0:T(8,128)S(1)}, u32[]{:S(2)}, u32[]{:S(2)}) %collective-permute-start.5) | collective-permute-done | bytes 524320 | tf_op jit(solution)/shard_map/ppermute | solution.py:9
  178.2 5.6 %collective-permute-done.4 = f32[256,512]{0,1:T(8,128)S(1)} collective-permute-done((f32[256,512]{0,1:T(8,128)}, f32[256,512]{0,1:T(8,128)S(1)}, u32[]{:S(2)}, u32[]{:S(2)}) %collective-permute-start.4) | collective-permute-done | bytes 524320 | tf_op jit(solution)/shard_map/ppermute | solution.py:21
  183.8 1.1 convolution_bitcast_fusion.2
  184.9 1.5 pad_maximum_fusion.4
  (26 shorter events, 6.0 us)
Async XLA Ops:
  6.5 21.5 %copy-start = (f32[1024,512]{1,0:T(8,128)S(1)}, f32[1024,512]{1,0:T(8,128)}, u32[]{:S(2)}) copy-start(f32[1024,512]{1,0:T(8,128)} %param.5) | copy-start | bytes 6291460
  6.5 21.5 %all-gather.5.cloned.1.call-start = ((), (), s32[]{:S(2)}) async-start(), calls=%async_computation | async-start | bytes 1310720 | tf_op jit(solution)/shard_map/all_gather | solution.py:49
  7.3 69.8 %all-gather.7.cloned.1.call-start = ((), (), s32[]{:S(2)}) async-start(), calls=%async_computation.1 | async-start | bytes 2359296 | tf_op jit(solution)/shard_map/all_gather | solution.py:51
  8.0 88.2 %all-gather.9.cloned.1.call-start = ((), (), s32[]{:S(2)}) async-start(), calls=%async_computation.2 | async-start | bytes 1310720 | tf_op jit(solution)/shard_map/all_gather | solution.py:53
  8.7 159.0 %all-gather.11.cloned.1.call-start = ((), (), s32[]{:S(2)}) async-start(), calls=%async_computation.3 | async-start | bytes 2359296 | tf_op jit(solution)/shard_map/all_gather | solution.py:64
  82.8 1.7 copy-start.1
  84.5 59.8 %collective-permute-start = (f32[1024,256]{1,0:T(8,128)S(1)}, f32[1024,256]{1,0:T(8,128)}, u32[]{:S(2)}, u32[]{:S(2)}) collective-permute-start(f32[1024,256]{1,0:T(8,128)S(1)} %get-tuple-element.7), channel_id=1, source_target_pairs={{0,1},{1,2},{2,3},{3,4},{4,5},{5,6},{6,7},{7,0},{8,9},{9,10},{10,1... | collective-permute-start | bytes 3145736 | tf_op jit(solution)/shard_map/ppermute | solution.py:19
  84.8 69.9 %collective-permute-start.1 = (f32[1024,256]{1,0:T(8,128)}, f32[1024,256]{1,0:T(8,128)}, u32[]{:S(2)}, u32[]{:S(2)}) collective-permute-start(f32[1024,256]{1,0:T(8,128)} %get-tuple-element.8), channel_id=1, source_target_pairs={{1,0},{2,1},{3,2},{4,3},{5,4},{6,5},{7,6},{0,7},{9,8},{10,9},{11,1... | collective-permute-start | bytes 3145736 | tf_op jit(solution)/shard_map/ppermute | solution.py:21
  97.3 57.4 %copy-start.2 = (f32[2,512,512]{1,2,0:T(8,128)S(1)}, f32[2,512,512]{1,2,0:T(8,128)}, u32[]{:S(2)}) copy-start(f32[2,512,512]{1,2,0:T(8,128)} %copy-done.1) | copy-start | bytes 6291460
  97.3 57.3 %collective-permute-start.2 = (f32[512,256]{1,0:T(8,128)S(1)}, f32[512,256]{1,0:T(8,128)S(1)}, u32[]{:S(2)}, u32[]{:S(2)}) collective-permute-start(f32[512,256]{1,0:T(8,128)S(1)} %slice.68), channel_id=1, source_target_pairs={{0,7},{1,0},{2,1},{3,2},{4,3},{5,4},{6,5},{7,6},{8,15},{9,8},{10,9... | collective-permute-start | bytes 1572872 | tf_op jit(solution)/shard_map/ppermute | solution.py:9
  157.9 1.0 copy-start.3
  159.9 12.8 %collective-permute-start.3 = (f32[256,512]{0,1:T(8,128)}, f32[256,512]{0,1:T(8,128)}, u32[]{:S(2)}, u32[]{:S(2)}) collective-permute-start(f32[256,512]{0,1:T(8,128)} %get-tuple-element.5), channel_id=1, source_target_pairs={{0,8},{8,16},{16,24},{24,0},{1,9},{9,17},{17,25},{25,1},{2,10},{10... | collective-permute-start | bytes 1572872 | tf_op jit(solution)/shard_map/ppermute | solution.py:19
  167.7 3.1 %copy-start.4 = (f32[1024,256]{0,1:T(8,128)S(1)}, f32[1024,256]{0,1:T(8,128)}, u32[]{:S(2)}) copy-start(f32[1024,256]{0,1:T(8,128)} %copy-done.3) | copy-start | bytes 3145732
  167.7 3.1 %copy-start.5 = (f32[2,512,512]{2,1,0:T(8,128)S(1)}, f32[2,512,512]{2,1,0:T(8,128)}, u32[]{:S(2)}) copy-start(f32[2,512,512]{2,1,0:T(8,128)} %all-gather.11.cloned.1.call-done) | copy-start | bytes 6291460
  169.2 9.0 %collective-permute-start.5 = (f32[512,256]{1,0:T(8,128)S(1)}, f32[512,256]{1,0:T(8,128)S(1)}, u32[]{:S(2)}, u32[]{:S(2)}) collective-permute-start(f32[512,256]{1,0:T(8,128)S(1)} %slice.74), channel_id=1, source_target_pairs={{0,24},{8,0},{16,8},{24,16},{1,25},{9,1},{17,9},{25,17},{2,26},{10... | collective-permute-start | bytes 1572872 | tf_op jit(solution)/shard_map/ppermute | solution.py:9
  170.2 13.6 %collective-permute-start.4 = (f32[256,512]{0,1:T(8,128)}, f32[256,512]{0,1:T(8,128)S(1)}, u32[]{:S(2)}, u32[]{:S(2)}) collective-permute-start(f32[256,512]{0,1:T(8,128)} %get-tuple-element.6), channel_id=1, source_target_pairs={{8,0},{16,8},{24,16},{0,24},{9,1},{17,9},{25,17},{1,25},{10,2},{18... | collective-permute-start | bytes 1572872 | tf_op jit(solution)/shard_map/ppermute | solution.py:21
Sparse Core Ops, SparseCore 0:
  8.9 19.1 all-gather.4
  30.3 46.7 all-gather.6
  78.6 17.5 all-gather.8
  98.2 69.4 all-gather.10
where the time goes:
time: 193 us
  waiting for transfers between devices  128 us (66%)
  matrix products  27.1 us (14%)
  starting transfers between devices  13.8 us (7%)
  between operations  13.2 us (7%)
  local copies, waits for them, and re-layouts  8.15 us (4%)
  other arithmetic  2.53 us (1%)
    ppermute x2, waiting for transfers between devices, padded_2(): lax.ppermute(tail, axis, [(i, (i + 1) % count) for i in range(count)])  42.8 us
    all_gather x1, waiting for transfers between devices, body(): rotations = lax.all_gather(left_rot, 'col', axis=1, tiled=True)  36.8 us
    all_gather x1, waiting for transfers between devices, body(): rotations = lax.all_gather(right_rot, 'row', axis=1, tiled=True)  18.8 us
    ppermute x2, waiting for transfers between devices, passed_along(): return lax.ppermute(x, axis, [(i, (i + by) % size) for i in range(size)])  9.97 us
    dot_general x1, matrix products, apply_right(): jnp.einsum('rka,kab->rkb', shaped, rotations, precision=lax.Precision.HIG...  9.25 us
    dot_general x2, matrix products, apply_left(): jnp.einsum('kab,kac->kbc', rotations, shaped, precision=lax.Precision.HIG...  7.62 us
    all_gather x1, waiting for transfers between devices, body(): rotations = lax.all_gather(right_off, 'row', axis=1, tiled=True)  7.54 us
    ppermute x2, waiting for transfers between devices, padded_2(): lax.ppermute(head, axis, [((i + 1) % count, i) for i in range(count)])  5.62 us
  transfers between devices with their start and end apart: 10, of which 8 were waited for; matrix products, arithmetic and copies ran while one was open for 18% of the time, Pallas kernels for 0%

commit v1 on v0

--- a/solution.py
+++ b/solution.py
@@ -2,6 +2,28 @@
 import jax.numpy as jnp
 from jax import lax
 from jax.sharding import PartitionSpec as P
+
+
+def joined_along(pieces, dim):
+    dims = list(pieces.shape[1:])
+    dims[dim] *= pieces.shape[0]
+    return jnp.moveaxis(pieces, 0, dim).reshape(dims)
+
+
+def ring_gather(shard, axis, dim):
+    length = lax.axis_size(axis)
+    pairs = [(i, (i + 1) % length) for i in range(length)]
+    back = [(b, a) for a, b in pairs]
+    lower, upper = ([], [])
+    for hop in range(length - 1):
+        if hop % 2 == 0:
+            lower.append(lax.ppermute(lower[-1] if lower else shard, axis, pairs))
+        else:
+            upper.append(lax.ppermute(upper[-1] if upper else shard, axis, back))
+    blocks = jnp.stack([*lower[::-1], shard, *upper])
+    shift = lax.axis_index(axis) - len(lower)
+    blocks = blocks[(jnp.arange(length) - shift) % length]
+    return joined_along(blocks, dim)
 
 
 def passed_along(x, axis, by):
@@ -46,7 +68,7 @@
     half_window = window // 2
     rows_here = schur.shape[0]
     cols_here = schur.shape[1]
-    rotations = lax.all_gather(right_rot, "row", axis=1, tiled=True)
+    rotations = ring_gather(right_rot, "row", 1)
     matrix = apply_right(schur, rotations)
     rotations = lax.all_gather(left_rot, "col", axis=1, tiled=True)
     matrix = apply_left(matrix, rotations)

time: 193 us -> 175 us (0.907)
  waiting for transfers between devices: 128 us -> 102 us
  starting transfers between devices: 13.8 us -> 18.8 us
  other arithmetic: 2.53 us -> 4.57 us
    all_gather x1 -> x0, waiting for transfers between devices: 18.8 us -> none  [body(): rotations = lax.all_gather(right_rot, 'row', axis=1, tiled=True)]
    all_gather x1, waiting for transfers between devices: 36.8 us -> 20.5 us  [body(): rotations = lax.all_gather(left_rot, 'col', axis=1, tiled=True)]
    ppermute x0 -> x3, waiting for transfers between devices: none -> 9.64 us  [the longest x2 9.64 us: ring_gather(): lower.append(lax.ppermute(lower[-1] if lower else shard, axis, pairs))]
    ppermute x0 -> x3, starting transfers between devices: none -> 5.02 us  [the longest x2 5.02 us: ring_gather(): lower.append(lax.ppermute(lower[-1] if lower else shard, axis, pairs))]
    another operation x0 -> x1, other arithmetic: none -> 2.02 us  [ring_gather(): blocks = jnp.stack([*lower[::-1], shard, *upper])]
  transfers between devices with their start and end apart: 10 -> 12, of which waited for: 8 -> 9; matrix products, arithmetic and copies ran while one was open for 18% -> 21% of each run, Pallas kernels for 0% -> 0%
where the time goes in v1:
time: 175 us
  waiting for transfers between devices  102 us (58%)
  matrix products  25.8 us (15%)
  starting transfers between devices  18.8 us (11%)
  between operations  13.2 us (8%)
  local copies, waits for them, and re-layouts  9.95 us (6%)
  other arithmetic  4.57 us (3%)
    ppermute x2, waiting for transfers between devices, padded_2(): lax.ppermute(tail, axis, [(i, (i + 1) % count) for i in range(count)])  42.8 us
    all_gather x1, waiting for transfers between devices, body(): rotations = lax.all_gather(left_rot, 'col', axis=1, tiled=True)  20.5 us
    ppermute x2, waiting for transfers between devices, passed_along(): return lax.ppermute(x, axis, [(i, (i + by) % size) for i in range(size)])  9.99 us
    ppermute x2, waiting for transfers between devices, ring_gather(): lower.append(lax.ppermute(lower[-1] if lower else shard, axis, pairs))  9.64 us
    dot_general x1, matrix products, apply_right(): jnp.einsum('rka,kab->rkb', shaped, rotations, precision=lax.Precision.HIG...  8.03 us
    dot_general x2, matrix products, apply_left(): jnp.einsum('kab,kac->kbc', rotations, shaped, precision=lax.Precision.HIG...  7.62 us
    all_gather x1, waiting for transfers between devices, body(): rotations = lax.all_gather(right_off, 'row', axis=1, tiled=True)  7.53 us
    ppermute x2, waiting for transfers between devices, padded_2(): lax.ppermute(head, axis, [((i + 1) % count, i) for i in range(count)])  5.62 us
  transfers between devices with their start and end apart: 12, of which 9 were waited for; matrix products, arithmetic and copies ran while one was open for 21% of the time, Pallas kernels for 0%

profile of v1, /device:TPU:1, one launch (start us, length us, event | category | flops | bytes accessed | tf_op | source)
XLA Modules:
  0.0 174.6 jit_solution(14104615874621838802)
XLA Ops:
  8.7 2.6 %collective-permute-start = (f32[1,128,512]{2,1,0:T(8,128)}, f32[1,128,512]{2,1,0:T(8,128)S(1)}, u32[]{:S(2)}, u32[]{:S(2)}) collective-permute-start(f32[1,128,512]{2,1,0:T(8,128)} %param.7), channel_id=1, source_target_pairs={{0,8},{8,16},{16,24},{24,0},{1,9},{9,17},{17,25},{25,1},{2,10},{10... | collective-permute-start | bytes 786440 | tf_op jit(solution)/shard_map/ppermute | solution.py:20
  11.4 6.4 %collective-permute-done = f32[1,128,512]{2,1,0:T(8,128)S(1)} collective-permute-done((f32[1,128,512]{2,1,0:T(8,128)}, f32[1,128,512]{2,1,0:T(8,128)S(1)}, u32[]{:S(2)}, u32[]{:S(2)}) %collective-permute-start) | collective-permute-done | bytes 262176 | tf_op jit(solution)/shard_map/ppermute | solution.py:20
  17.7 2.4 %collective-permute-start.1 = (f32[1,128,512]{2,1,0:T(8,128)S(1)}, f32[1,128,512]{2,1,0:T(8,128)S(1)}, u32[]{:S(2)}, u32[]{:S(2)}) collective-permute-start(f32[1,128,512]{2,1,0:T(8,128)S(1)} %collective-permute-done), channel_id=1, source_target_pairs={{0,8},{8,16},{16,24},{24,0},{1,9},{9,17},{17,25},{25,1},{2,10},{10... | collective-permute-start | bytes 786440 | tf_op jit(solution)/shard_map/ppermute | solution.py:20
  20.2 3.3 %collective-permute-done.1 = f32[1,128,512]{2,1,0:T(8,128)S(1)} collective-permute-done((f32[1,128,512]{2,1,0:T(8,128)S(1)}, f32[1,128,512]{2,1,0:T(8,128)S(1)}, u32[]{:S(2)}, u32[]{:S(2)}) %collective-permute-start.1) | collective-permute-done | bytes 262176 | tf_op jit(solution)/shard_map/ppermute | solution.py:20
  23.4 2.0 %maximum_bitcast_fusion = f32[4,128,512]{2,1,0:T(8,128)} fusion(f32[1,1,128,512]{3,2,1,0:T(8,128)S(1)} %bitcast.44, f32[1,1,128,512]{3,2,1,0:T(8,128)} %bitcast.42, f32[1,1,128,512]{3,2,1,0:T(8,128)S(1)} %bitcast.43, f32[1,1,128,512]{3,2,1,0:T(8,128)S(1)} %bitcast.45), kind=kLoop, calls=%fused_computation.23 | loop fusion | flops 786432 | bytes 2097152 | tf_op jit(solution)/shard_map/stack | solution.py:23
  25.5 1.8 %gather_fusion = f32[4,128,512]{2,1,0:T(8,128)S(1)} fusion(f32[4,128,512]{2,1,0:T(8,128)} %maximum_bitcast_fusion, s32[1024]{0:T(1024)S(1)} %pad_clamp_fusion), kind=kCustom, calls=%fused_computation | custom fusion | bytes 2097168 | tf_op jit(solution)/shard_map/gather | solution.py:25
  27.3 8.0 %convolution_bitcast_fusion = f32[1024,1,512]{0,2,1:T(8,128)} fusion(f32[512,512]{1,0:T(8,128)S(1)} %bitcast.39, f32[1024,512]{1,0:T(8,128)S(1)} %copy-done), kind=kOutput, calls=%fused_computation.10 | convolution fusion | flops 3221225472 | bytes 5242880 | tf_op jit(solution)/shard_map/rka,kab->rkb/dot_general | solution.py:62
  35.3 2.9 %copy.7 = f32[1024,1,512]{2,0,1:T(8,128)} copy(f32[1024,1,512]{0,2,1:T(8,128)} %convolution_bitcast_fusion) | data formatting | bytes 4194304 | tf_op jit(solution)/shard_map/reshape;reshape | solution.py:53
  38.3 20.5 %all-gather.4.cloned.1.call-done = f32[2,512,512]{2,1,0:T(8,128)} async-done(((f32[2,64,512]{2,1,0:T(8,128)}), f32[2,512,512]{2,1,0:T(8,128)}) %all-gather.4.cloned.1.call-update) | async-done | bytes 2097168 | tf_op jit(solution)/shard_map/all_gather | solution.py:73
  58.8 5.8 %fusion.18 = f32[2,512,512]{1,2,0:T(8,128)S(1)} fusion(f32[2,512,512]{2,1,0:T(8,128)} %bitcast.38, f32[2,512,512]{2,1,0:T(8,128)} %all-gather.4.cloned.1.call-done), kind=kOutput, calls=%fused_computation.41 | convolution fusion | flops 3221225472 | bytes 6291456 | tf_op jit(solution)/shard_map/kab,kac->kbc/dot_general | solution.py:54
  66.5 3.9 %collective-permute-start.4 = (f32[1024,256]{1,0:T(8,128)}, f32[1024,256]{1,0:T(8,128)}, u32[]{:S(2)}, u32[]{:S(2)}) collective-permute-start(f32[1024,256]{1,0:T(8,128)} %get-tuple-element.8), channel_id=1, source_target_pairs={{1,0},{2,1},{3,2},{4,3},{5,4},{6,5},{7,6},{0,7},{9,8},{10,9},{11,1... | collective-permute-start | bytes 3145736 | tf_op jit(solution)/shard_map/ppermute | solution.py:43
  70.4 7.5 %all-gather.6.cloned.1.call-done = f32[1,512,512]{2,1,0:T(8,128)} async-done(((f32[1,128,512]{2,1,0:T(8,128)}), f32[1,512,512]{2,1,0:T(8,128)}) %all-gather.6.cloned.1.call-update) | async-done | bytes 1048592 | tf_op jit(solution)/shard_map/all_gather | solution.py:75
  79.0 4.2 %collective-permute-start.5 = (f32[512,256]{1,0:T(8,128)S(1)}, f32[512,256]{1,0:T(8,128)S(1)}, u32[]{:S(2)}, u32[]{:S(2)}) collective-permute-start(f32[512,256]{1,0:T(8,128)S(1)} %slice.70), channel_id=1, source_target_pairs={{0,7},{1,0},{2,1},{3,2},{4,3},{5,4},{6,5},{7,6},{8,15},{9,8},{10,9... | collective-permute-start | bytes 1572872 | tf_op jit(solution)/shard_map/ppermute | solution.py:31
  83.2 42.8 %collective-permute-done.3 = f32[1024,256]{1,0:T(8,128)} collective-permute-done((f32[1024,256]{1,0:T(8,128)S(1)}, f32[1024,256]{1,0:T(8,128)}, u32[]{:S(2)}, u32[]{:S(2)}) %collective-permute-start.3) | collective-permute-done | bytes 1048608 | tf_op jit(solution)/shard_map/ppermute | solution.py:41
  126.0 3.6 %fusion.2 = f32[1024,256]{0,1:T(8,128)S(1)} fusion(f32[1024,512]{1,0:T(8,128)} %bitcast.36, f32[1024,256]{1,0:T(8,128)} %collective-permute-done.3, f32[512,512]{1,0:T(8,128)} %bitcast.41), kind=kOutput, calls=%fused_computation.5 | convolution fusion | flops 1611137024 | bytes 4718592 | tf_op jit(solution)/shard_map/dot_general | solution.py:78
  129.6 6.7 %collective-permute-done.5 = f32[512,256]{1,0:T(8,128)S(1)} collective-permute-done((f32[512,256]{1,0:T(8,128)S(1)}, f32[512,256]{1,0:T(8,128)S(1)}, u32[]{:S(2)}, u32[]{:S(2)}) %collective-permute-start.5) | collective-permute-done | bytes 524320 | tf_op jit(solution)/shard_map/ppermute | solution.py:31
  136.3 3.3 %fusion = f32[1024,256]{0,1:T(8,128)S(1)} fusion(f32[512,256]{1,0:T(8,128)S(1)} %collective-permute-done.5, f32[1024,256]{1,0:T(8,128)} %collective-permute-done.4, f32[1024,512]{1,0:T(8,128)S(1)} %bitcast.37), kind=kOutput, calls=%fused_computation.2 | convolution fusion | flops 1611137024 | bytes 4718592 | tf_op jit(solution)/shard_map/dot_general | solution.py:82
  141.6 3.7 %collective-permute-start.6 = (f32[256,512]{0,1:T(8,128)}, f32[256,512]{0,1:T(8,128)}, u32[]{:S(2)}, u32[]{:S(2)}) collective-permute-start(f32[256,512]{0,1:T(8,128)} %get-tuple-element.5), channel_id=1, source_target_pairs={{0,8},{8,16},{16,24},{24,0},{1,9},{9,17},{17,25},{25,1},{2,10},{10... | collective-permute-start | bytes 1572872 | tf_op jit(solution)/shard_map/ppermute | solution.py:41
  145.4 4.1 %all-gather.8.cloned.1.call-done = f32[2,512,512]{2,1,0:T(8,128)} async-done(((f32[2,64,512]{2,1,0:T(8,128)}), f32[2,512,512]{2,1,0:T(8,128)}) %all-gather.8.cloned.1.call-update) | async-done | bytes 2097168 | tf_op jit(solution)/shard_map/all_gather | solution.py:86
  152.6 1.9 %convolution_bitcast_fusion.1 = f32[512,512]{1,0:T(8,128)S(1)} fusion(f32[1024,256]{0,1:T(8,128)S(1)} %fusion.2, f32[1024,256]{0,1:T(8,128)S(1)} %copy-done.4, f32[2,512,512]{2,1,0:T(8,128)S(1)} %copy-done.5), kind=kOutput, calls=%fused_computation.11 | convolution fusion | flops 1610874880 | bytes 4194304 | tf_op jit(solution)/shard_map/kab,kac->kbc/dot_general | solution.py:54
  154.4 2.1 %convolution_bitcast_fusion.3 = f32[256,512]{1,0:T(8,128)S(1)} fusion(f32[256,512]{0,1:T(8,128)} %collective-permute-done.6, f32[1024,256]{0,1:T(8,128)S(1)} %copy-done.4, f32[1024,256]{0,1:T(8,128)S(1)} %fusion.2, f32[512,512]{1,0:T(8,128)S(1)} %slice_bitcast_fusion.2), kind=kOutput, calls=%fused_computation.13 | convolution fusion | flops 805830656 | bytes 3670016 | tf_op jit(solution)/shard_map/dot_general | solution.py:89
  156.6 3.3 %collective-permute-done.8 = f32[512,256]{1,0:T(8,128)S(1)} collective-permute-done((f32[512,256]{1,0:T(8,128)S(1)}, f32[512,256]{1,0:T(8,128)S(1)}, u32[]{:S(2)}, u32[]{:S(2)}) %collective-permute-start.8) | collective-permute-done | bytes 524320 | tf_op jit(solution)/shard_map/ppermute | solution.py:31
  159.9 5.6 %collective-permute-done.7 = f32[256,512]{0,1:T(8,128)S(1)} collective-permute-done((f32[256,512]{0,1:T(8,128)}, f32[256,512]{0,1:T(8,128)S(1)}, u32[]{:S(2)}, u32[]{:S(2)}) %collective-permute-start.7) | collective-permute-done | bytes 524320 | tf_op jit(solution)/shard_map/ppermute | solution.py:43
  166.6 1.5 pad_maximum_fusion.4
  (33 shorter events, 11.4 us)
Async XLA Ops:
  6.5 20.8 %copy-start = (f32[1024,512]{1,0:T(8,128)S(1)}, f32[1024,512]{1,0:T(8,128)}, u32[]{:S(2)}) copy-start(f32[1024,512]{1,0:T(8,128)} %param.5) | copy-start | bytes 6291460
  6.5 52.2 %all-gather.4.cloned.1.call-start = ((), (), s32[]{:S(2)}) async-start(), calls=%async_computation | async-start | bytes 2359296 | tf_op jit(solution)/shard_map/all_gather | solution.py:73
  7.3 70.6 %all-gather.6.cloned.1.call-start = ((), (), s32[]{:S(2)}) async-start(), calls=%async_computation.1 | async-start | bytes 1310720 | tf_op jit(solution)/shard_map/all_gather | solution.py:75
  8.0 141.4 %all-gather.8.cloned.1.call-start = ((), (), s32[]{:S(2)}) async-start(), calls=%async_computation.2 | async-start | bytes 2359296 | tf_op jit(solution)/shard_map/all_gather | solution.py:86
  8.7 9.0 %collective-permute-start = (f32[1,128,512]{2,1,0:T(8,128)}, f32[1,128,512]{2,1,0:T(8,128)S(1)}, u32[]{:S(2)}, u32[]{:S(2)}) collective-permute-start(f32[1,128,512]{2,1,0:T(8,128)} %param.7), channel_id=1, source_target_pairs={{0,8},{8,16},{16,24},{24,0},{1,9},{9,17},{17,25},{25,1},{2,10},{10... | collective-permute-start | bytes 786440 | tf_op jit(solution)/shard_map/ppermute | solution.py:20
  11.4 8.8 %collective-permute-start.2 = (f32[1,128,512]{2,1,0:T(8,128)}, f32[1,128,512]{2,1,0:T(8,128)S(1)}, u32[]{:S(2)}, u32[]{:S(2)}) collective-permute-start(f32[1,128,512]{2,1,0:T(8,128)} %param.7), channel_id=1, source_target_pairs={{8,0},{16,8},{24,16},{0,24},{9,1},{17,9},{25,17},{1,25},{10,2},{18... | collective-permute-start | bytes 786440 | tf_op jit(solution)/shard_map/ppermute | solution.py:22
  17.7 5.7 %collective-permute-start.1 = (f32[1,128,512]{2,1,0:T(8,128)S(1)}, f32[1,128,512]{2,1,0:T(8,128)S(1)}, u32[]{:S(2)}, u32[]{:S(2)}) collective-permute-start(f32[1,128,512]{2,1,0:T(8,128)S(1)} %collective-permute-done), channel_id=1, source_target_pairs={{0,8},{8,16},{16,24},{24,0},{1,9},{9,17},{17,25},{25,1},{2,10},{10... | collective-permute-start | bytes 786440 | tf_op jit(solution)/shard_map/ppermute | solution.py:20
  64.5 1.7 copy-start.1
  66.2 59.8 %collective-permute-start.3 = (f32[1024,256]{1,0:T(8,128)S(1)}, f32[1024,256]{1,0:T(8,128)}, u32[]{:S(2)}, u32[]{:S(2)}) collective-permute-start(f32[1024,256]{1,0:T(8,128)S(1)} %get-tuple-element.7), channel_id=1, source_target_pairs={{0,1},{1,2},{2,3},{3,4},{4,5},{5,6},{6,7},{7,0},{8,9},{9,10},{10,1... | collective-permute-start | bytes 3145736 | tf_op jit(solution)/shard_map/ppermute | solution.py:41
  66.5 69.9 %collective-permute-start.4 = (f32[1024,256]{1,0:T(8,128)}, f32[1024,256]{1,0:T(8,128)}, u32[]{:S(2)}, u32[]{:S(2)}) collective-permute-start(f32[1024,256]{1,0:T(8,128)} %get-tuple-element.8), channel_id=1, source_target_pairs={{1,0},{2,1},{3,2},{4,3},{5,4},{6,5},{7,6},{0,7},{9,8},{10,9},{11,1... | collective-permute-start | bytes 3145736 | tf_op jit(solution)/shard_map/ppermute | solution.py:43
  79.0 57.4 %copy-start.2 = (f32[2,512,512]{1,2,0:T(8,128)S(1)}, f32[2,512,512]{1,2,0:T(8,128)}, u32[]{:S(2)}) copy-start(f32[2,512,512]{1,2,0:T(8,128)} %copy-done.1) | copy-start | bytes 6291460
  79.0 57.3 %collective-permute-start.5 = (f32[512,256]{1,0:T(8,128)S(1)}, f32[512,256]{1,0:T(8,128)S(1)}, u32[]{:S(2)}, u32[]{:S(2)}) collective-permute-start(f32[512,256]{1,0:T(8,128)S(1)} %slice.70), channel_id=1, source_target_pairs={{0,7},{1,0},{2,1},{3,2},{4,3},{5,4},{6,5},{7,6},{8,15},{9,8},{10,9... | collective-permute-start | bytes 1572872 | tf_op jit(solution)/shard_map/ppermute | solution.py:31
  139.6 1.0 copy-start.3
  141.6 12.8 %collective-permute-start.6 = (f32[256,512]{0,1:T(8,128)}, f32[256,512]{0,1:T(8,128)}, u32[]{:S(2)}, u32[]{:S(2)}) collective-permute-start(f32[256,512]{0,1:T(8,128)} %get-tuple-element.5), channel_id=1, source_target_pairs={{0,8},{8,16},{16,24},{24,0},{1,9},{9,17},{17,25},{25,1},{2,10},{10... | collective-permute-start | bytes 1572872 | tf_op jit(solution)/shard_map/ppermute | solution.py:41
  149.4 3.1 %copy-start.4 = (f32[1024,256]{0,1:T(8,128)S(1)}, f32[1024,256]{0,1:T(8,128)}, u32[]{:S(2)}) copy-start(f32[1024,256]{0,1:T(8,128)} %copy-done.3) | copy-start | bytes 3145732
  149.4 3.1 %copy-start.5 = (f32[2,512,512]{2,1,0:T(8,128)S(1)}, f32[2,512,512]{2,1,0:T(8,128)}, u32[]{:S(2)}) copy-start(f32[2,512,512]{2,1,0:T(8,128)} %all-gather.8.cloned.1.call-done) | copy-start | bytes 6291460
  150.9 9.0 %collective-permute-start.8 = (f32[512,256]{1,0:T(8,128)S(1)}, f32[512,256]{1,0:T(8,128)S(1)}, u32[]{:S(2)}, u32[]{:S(2)}) collective-permute-start(f32[512,256]{1,0:T(8,128)S(1)} %slice.76), channel_id=1, source_target_pairs={{0,24},{8,0},{16,8},{24,16},{1,25},{9,1},{17,9},{25,17},{2,26},{10... | collective-permute-start | bytes 1572872 | tf_op jit(solution)/shard_map/ppermute | solution.py:31
  151.9 13.6 %collective-permute-start.7 = (f32[256,512]{0,1:T(8,128)}, f32[256,512]{0,1:T(8,128)S(1)}, u32[]{:S(2)}, u32[]{:S(2)}) collective-permute-start(f32[256,512]{0,1:T(8,128)} %get-tuple-element.6), channel_id=1, source_target_pairs={{8,0},{16,8},{24,16},{0,24},{9,1},{17,9},{25,17},{1,25},{10,2},{18... | collective-permute-start | bytes 1572872 | tf_op jit(solution)/shard_map/ppermute | solution.py:43
Sparse Core Ops, SparseCore 0:
  9.5 49.2 all-gather.3
  60.3 17.5 all-gather.5
  80.1 69.2 all-gather.7
